TPU v7x, 32 devices: a whole 2x2x4 slice. The times are simulated.
32 devices in a mesh: chan: 2 (over x), ctx: 16 (over z, y, core).
Axes of the slice: x: 2, y: 2, z: 4, core: 2. Of those that a mesh axis runs over, the one named last changes fastest.
Arguments:
- value: bfloat16 [2, 2048, 2048], P(None, 'ctx', 'chan'), may hold values from -6 to 6
- gate_in: bfloat16 [2, 2048, 2048], P(None, 'ctx', 'chan'), may hold values from -6 to 6
- gate_out: bfloat16 [2, 2048, 2048], P(None, 'ctx', 'chan'), may hold values from -6 to 6
- filters: float32 [384, 2048], P(None, 'chan'), may hold values from -0.3125 to 0.3125
- skip: float32 [2048], P('chan'), may hold values from -5 to 5
- proj: bfloat16 [2048, 2048], P(('chan', 'ctx')), may hold values from -0.125 to 0.125
- taps: float32 [128, 2048], P(None, 'chan'), may hold values from -0.5 to 0.5
Outputs:
- result: bfloat16 [2, 2048, 2048], P(None, 'ctx', 'chan')
All inputs are finite; a program needn't handle non-finite values.
Results may differ from a plain program's by a relative error of at most 0.0057.
Values may be sent and summed in bfloat16 or wider, within the bound.
A program may use at most 128 MiB of HBM per device.

v0:
```python
import functools
import math

import jax
import jax.numpy as jnp
import numpy as np
from jax import lax
from jax.experimental import pallas as pl
from jax.experimental.pallas import tpu as pltpu
from jax.sharding import PartitionSpec as P

F32 = jnp.float32
BF16 = jnp.bfloat16


def split(x):
    high = x.astype(BF16)
    return high, (x - high.astype(F32)).astype(BF16)


def split_table(table):
    high = table.astype(BF16)
    return high, (table - high.astype(np.float64)).astype(BF16)


def tables(rows):
    size = 2 * rows
    product = (2 * np.arange(rows)[:, None] + 1) * np.arange(size)[None, :] % (2 * size)
    phase = product * (math.pi / size)
    forward = np.concatenate([np.cos(phase), -np.sin(phase)], axis=0)
    inverse = forward[:, rows:].T * (2.0 / size)
    return (*split_table(forward), *split_table(np.ascontiguousarray(inverse)))


def mm(left, right):
    return jnp.dot(left, right, preferred_element_type=F32)


def lag_spectrum(lags, fwd_hi, fwd_lo):
    rows = lags.shape[0]
    high, low = split(lags)
    return mm(fwd_hi[:, :rows], high) + mm(fwd_hi[:, :rows], low) + mm(fwd_lo[:, :rows], high)


def convolve(windows, spectra, table_refs):
    fwd_hi, fwd_lo, inv_hi, inv_lo = table_refs
    total_re = total_im = None
    for window, spectrum in zip(windows, spectra):
        seen = mm(fwd_hi[...], window) + mm(fwd_lo[...], window)
        half = seen.shape[0] // 2
        x_re, x_im, h_re, h_im = seen[:half], seen[half:], spectrum[:half], spectrum[half:]
        re = x_re * h_re - x_im * h_im
        im = x_re * h_im + x_im * h_re
        total_re = re if total_re is None else total_re + re
        total_im = im if total_im is None else total_im + im
    high, low = split(jnp.concatenate([total_re, total_im], axis=0))
    return mm(inv_hi[...], high) + mm(inv_hi[...], low) + mm(inv_lo[...], high)


def mix_kernel(fh, fl, ih, il, filters, skip, gate, *rest):
    blocks, out = rest[:-1], rest[-1]
    batch, rows, _ = out.shape
    count = filters.shape[0] // rows
    spectra = [
        lag_spectrum(filters[s * rows : (s + 1) * rows], fh[...], fl[...]) for s in range(count)
    ]
    for b in range(batch):
        windows = [
            jnp.concatenate([blocks[s + 1][b], blocks[s][b]], axis=0) for s in range(count)
        ]
        conv = convolve(windows, spectra, (fh, fl, ih, il))
        own = blocks[0][b].astype(F32)
        out[b] = (gate[b].astype(F32) * (conv + skip[...] * own)).astype(BF16)


def filter_kernel(fh, fl, ih, il, taps, gate, behind, own, out):
    spectra = [lag_spectrum(taps[...], fh[...], fl[...])]
    for b in range(out.shape[0]):
        window = jnp.concatenate([behind[b], own[b]], axis=0)
        shorted = convolve([window], spectra, (fh, fl, ih, il))
        out[b] = (gate[b].astype(F32) * shorted).astype(BF16)


def tiled(kernel, consts, rows_args, block_args, tile, flops):
    batch, rows, channels = block_args[0].shape
    whole = lambda a: pl.BlockSpec(a.shape, lambda i: (0, 0))
    across = lambda a: pl.BlockSpec((a.shape[0], tile), lambda i: (0, i))
    block = pl.BlockSpec((batch, rows, tile), lambda i: (0, 0, i))
    args = [*consts, *rows_args, *block_args]
    return pl.pallas_call(
        kernel,
        grid=(channels // tile,),
        in_specs=[whole(a) for a in consts]
        + [across(a) for a in rows_args]
        + [block for _ in block_args],
        out_specs=block,
        out_shape=jax.ShapeDtypeStruct((batch, rows, channels), BF16),
        cost_estimate=pl.CostEstimate(
            flops=flops,
            bytes_accessed=sum(a.size * a.dtype.itemsize for a in args),
            transcendentals=0,
        ),
    )(*args)


def from_behind(value, steps):
    count = lax.axis_size("ctx")
    return lax.ppermute(value, "ctx", [(s, s + steps) for s in range(count - steps)])


MESH = pl.DeviceIdType.MESH


def fused_kernel(
    value_any, proj_any, fh_any, fl_any, ih_any, il_any, skip_any, filters_any, taps_any,
    gate_in_any, gate_out_any,
    out_any,
    value, fh, fl, ih, il, skip, out,
    past, gathered, mixed, spectra, tap_spectra, filters, taps, gate_in, gate_out,
    x_send, x_recv, own_rows, rim,
    load_sem, store_sem, own_sem, back_send, back_recv, halo_send, halo_recv, relay_send, relay_recv, far_send, far_recv,
    near_send, near_recv, ring_send, ring_recv, share_send, share_recv,
    x_send_sem, x_recv_sem, rim_send, rim_recv,
):
    batch, rows, channels = value.shape
    count = lax.axis_size("ctx")
    chips = count // 2
    evens = chips // 2
    half = gathered.shape[-1]
    tile = min(256, half)
    me, j = lax.axis_index("chan"), lax.axis_index("ctx")
    chip, core = j // 2, j % 2
    sibling = chip * 2 + 1 - core
    partner = 1 - me
    place = jnp.where(chip % 2 == 0, chip // 2, chips - 1 - chip // 2)

    def holder(position):
        position = (position + chips) % chips
        number = jnp.where(position < evens, 2 * position, 2 * (chips - 1 - position) + 1)
        return number * 2 + core

    loads = [
        pltpu.make_async_copy(a, b, load_sem.at[i])
        for i, (a, b) in enumerate(
            [
                (filters_any, filters),
                (taps_any, taps),
                (gate_in_any, gate_in),
                (gate_out_any, gate_out),
                (fh_any, fh),
                (fl_any, fl),
                (ih_any, ih),
                (il_any, il),
                (skip_any, skip),
                (value_any, value),
            ]
        )
    ]
    for load in loads:
        load.start()

    def columns(unit):
        owner = partner if unit < 2 else me
        start = owner * (2 * half) + (unit % 2) * half
        return pl.ds(pl.multiple_of(start, half), half)

    own_copies = [
        pltpu.make_async_copy(proj_any.at[:, columns(q)], gathered.at[q, j], own_sem.at[q])
        for q in range(4)
    ]
    for copy in own_copies:
        copy.start()

    barrier = pltpu.get_barrier_semaphore()
    following, preceding = holder(place + 1), holder(place - 1)
    expected = 3
    for peer in ((me, following), (me, preceding), (partner, j)):
        pl.semaphore_signal(barrier, inc=1, device_id=peer, device_id_type=MESH)
    for offset in (-3, -2, -1, 1, 2, 3):
        there = (j + offset >= 0) & (j + offset < count)
        expected = expected + there.astype(jnp.int32)

        @pl.when(there)
        def _(offset=offset):
            pl.semaphore_signal(barrier, inc=1, device_id=(me, j + offset), device_id_type=MESH)

    pl.semaphore_wait(barrier, expected)

    def remote(source, target, send_sem, recv_sem, peer):
        return pltpu.make_async_remote_copy(
            src_ref=source,
            dst_ref=target,
            send_sem=send_sem,
            recv_sem=recv_sem,
            device_id=peer,
            device_id_type=MESH,
        )

    def halo(b):
        return remote(value_any.at[b], past.at[1, b], halo_send.at[b], halo_recv.at[b], (me, j + 2))

    def far(b):
        return remote(value_any.at[b], past.at[2, b], far_send.at[b], far_recv.at[b], (me, j + 3))

    def near(b):
        return remote(value_any.at[b], past.at[0, b], near_send.at[b], near_recv.at[b], (me, sibling))

    def relay(b, slot):
        return remote(
            past.at[1, b], past.at[slot, b], relay_send.at[b], relay_recv.at[b], (me, sibling)
        )

    def back(b):
        return remote(past.at[2, b], past.at[1, b], back_send.at[b], back_recv.at[b], (me, j - 1))

    first, second = core == 0, core == 1
    even, odd = chip % 2 == 0, chip % 2 == 1
    has_behind = j >= 2
    sends_halo, gets_halo = (j + 2 < count) & (even | first), (j >= 2) & (odd | first)
    sends_far, gets_far = second & (j + 3 < count), first & (j >= 3)
    sends_back, gets_back = first & odd & (j >= 3), second & even & (j >= 2)

    def start_halo(b):
        @pl.when(sends_far)
        def _():
            far(b).start()

        @pl.when(sends_halo)
        def _():
            halo(b).start()

        @pl.when(first)
        def _():
            near(b).start()

    sent = []

    def begin(copy):
        copy.start()
        sent.append(copy)

    reach = chips // 2

    def steps(unit, direction):
        return reach if direction == 1 else chips - 1 - reach

    def slot(direction, step):
        return step if direction == 1 else reach + step

    def hop(unit, direction, step):
        origin = holder(place - direction * (step - 1))
        source = proj_any.at[:, columns(unit)] if step == 1 else gathered.at[unit, origin]
        k = slot(direction, step)
        return remote(
            source,
            gathered.at[unit, origin],
            ring_send.at[unit, k],
            ring_recv.at[unit, k],
            (me, following if direction == 1 else preceding),
        )

    def share(unit, direction, step):
        origin = holder(place - direction * step)
        k = slot(direction, step) if step else 0
        source = gathered.at[unit, origin] if step else proj_any.at[:, columns(unit)]
        return remote(
            source,
            gathered.at[unit, origin],
            share_send.at[unit, k],
            share_recv.at[unit, k],
            (me, sibling),
        )

    hops = {}

    def send_step(units, step):
        for unit in units:
            for direction in (1, -1):
                if step > 1 and step - 1 <= steps(unit, direction):
                    arrived = hops[unit, direction, step - 1]
                    arrived.wait_recv()
                if step <= steps(unit, direction):
                    copy = hops[unit, direction, step] = hop(unit, direction, step)
                    begin(copy)
                if step > 1 and step - 1 <= steps(unit, direction):
                    begin(share(unit, direction, step - 1))

    def finish(unit):
        own_copies[unit].wait()
        share(unit, 1, 0).wait_recv()
        for direction in (1, -1):
            for step in range(1, steps(unit, direction) + 1):
                k_origin = holder(place - direction * step)
                other = k_origin + 1 - 2 * core
                k = slot(direction, step)
                remote(
                    gathered.at[unit, other],
                    gathered.at[unit, other],
                    share_send.at[unit, k],
                    share_recv.at[unit, k],
                    (me, sibling),
                ).wait_recv()

    def product(unit):
        table = gathered[unit].reshape(count * proj_any.shape[0], half)
        return mm(mixed[...], table)

    start_halo(0)
    send_step((0, 1), 1)
    start_halo(1)
    send_step((2, 3), 1)
    for unit in range(4):
        begin(share(unit, 1, 0))

    table_refs = (fh, fl, ih, il)
    for load in (loads[0], *loads[4:]):
        load.wait()

    @pl.loop(0, channels // tile)
    def _(i):
        at = pl.ds(pl.multiple_of(i * tile, tile), tile)
        for s in range(spectra.shape[0]):
            spectra[s, :, at] = lag_spectrum(filters[s * rows : (s + 1) * rows, at], fh[...], fl[...])

    @pl.when(j < 2)
    def _():
        past[1] = jnp.zeros(past.shape[1:], BF16)

    @pl.when((j < 2) & first)
    def _():
        past[0] = jnp.zeros(past.shape[1:], BF16)

    @pl.when((j < 2) & second | (j < 3) & first)
    def _():
        past[2] = jnp.zeros(past.shape[1:], BF16)

    def relay_halo(b):
        @pl.when(gets_far)
        def _():
            far(b).wait_recv()

        @pl.when(sends_back)
        def _():
            back(b).start()

        @pl.when(gets_halo)
        def _():
            halo(b).wait_recv()

        @pl.when(gets_back)
        def _():
            back(b).wait_recv()

        @pl.when(has_behind & first)
        def _():
            relay(b, 2).start()

        @pl.when(has_behind & second)
        def _():
            relay(b, 0).start()

    relay_halo(0)
    send_step((0, 1), 2)
    relay_halo(1)
    send_step((2, 3), 2)
    loads[2].wait()

    def mix(b):
        @pl.when(second)
        def _():
            near(b).wait_recv()

        @pl.when(has_behind & first)
        def _():
            relay(b, 0).wait_recv()

        @pl.when(has_behind & second)
        def _():
            relay(b, 2).wait_recv()

        @pl.loop(0, channels // tile)
        def _(i):
            at = pl.ds(pl.multiple_of(i * tile, tile), tile)
            parts = [value[b, :, at]] + [past[s, b, :, at] for s in range(3)]
            windows = [jnp.concatenate([parts[s + 1], parts[s]], axis=0) for s in range(3)]
            conv = convolve(windows, [spectra.at[s, :, at][...] for s in range(3)], table_refs)
            both = conv + skip[:, at] * parts[0].astype(F32)
            gated = gate_in[b, :, at].astype(F32) * both
            mixed[b * rows : (b + 1) * rows, at] = gated.astype(BF16)

    mix(0)
    send_step((0, 1), 3)
    mix(1)
    send_step((2, 3), 3)
    send_step((0, 1), 4)
    loads[1].wait()

    @pl.loop(0, channels // tile)
    def _(i):
        at = pl.ds(pl.multiple_of(i * tile, tile), tile)
        tap_spectra[:, at] = lag_spectrum(taps[:, at], fh[...], fl[...])

    x_copies = []
    send_step((2, 3), 4)
    for step in range(5, reach + 2):
        send_step((0, 1), step)
    for unit in range(2):
        finish(unit)
        x_send[unit] = product(unit).astype(BF16)
        copy = remote(
            x_send.at[unit],
            x_recv.at[unit],
            x_send_sem.at[unit],
            x_recv_sem.at[unit],
            (partner, j),
        )
        x_copies.append(copy)
        begin(copy)
    for step in range(5, reach + 2):
        send_step((2, 3), step)

    @pl.when(j == 0)
    def _():
        rim[...] = jnp.zeros(rim.shape, BF16)

    def edge(h):
        return remote(
            own_rows.at[h], rim.at[h], rim_send.at[h], rim_recv.at[h], (me, j + 1)
        )

    for h in range(2):
        finish(2 + h)
        partial = product(2 + h)
        x_copies[h].wait_recv()
        total = (partial + x_recv[h].astype(F32)).astype(BF16)
        own_rows[h] = total.reshape(batch, rows, half)

        @pl.when(j + 1 < count)
        def _(h=h):
            edge(h).start()

    loads[3].wait()

    def store(h):
        part = pl.ds(h * half, half)
        return pltpu.make_async_copy(
            out.at[:, :, part], out_any.at[:, :, part], store_sem.at[h]
        )

    for h in range(2):

        @pl.when(j >= 1)
        def _(h=h):
            edge(h).wait_recv()

        @pl.loop(0, half // tile)
        def _(i, h=h):
            at = pl.ds(pl.multiple_of(i * tile, tile), tile)
            wide = pl.ds(pl.multiple_of(h * half + i * tile, tile), tile)
            spectrum = tap_spectra[:, wide]
            for b in range(batch):
                window = jnp.concatenate([rim[h, b, :, at], own_rows[h, b, :, at]], axis=0)
                shorted = convolve([window], [spectrum], table_refs)
                out[b, :, wide] = (gate_out[b, :, wide].astype(F32) * shorted).astype(BF16)

        store(h).start()

    for h in range(2):
        store(h).wait()
    for copy in sent:
        copy.wait_send()

    for b in range(batch):

        @pl.when(sends_halo)
        def _(b=b):
            halo(b).wait_send()

        @pl.when(first)
        def _(b=b):
            near(b).wait_send()

        @pl.when(sends_far)
        def _(b=b):
            far(b).wait_send()

        @pl.when(has_behind)
        def _(b=b):
            relay(b, 0).wait_send()

        @pl.when(sends_back)
        def _(b=b):
            back(b).wait_send()

    for h in range(2):

        @pl.when(j + 1 < count)
        def _(h=h):
            edge(h).wait_send()


def fused(value, gate_in, gate_out, filters, skip, proj, taps):
    batch, rows, channels = value.shape
    count = lax.axis_size("ctx")
    consts = [jnp.asarray(t) for t in tables(rows)]
    half = channels // 2
    slots = 2 * (count // 4) + 1
    dma = pltpu.SemaphoreType.DMA
    anywhere = pl.BlockSpec(memory_space=pl.ANY)
    return pl.pallas_call(
        fused_kernel,
        out_shape=jax.ShapeDtypeStruct(value.shape, BF16),
        in_specs=[anywhere] * 11,
        out_specs=anywhere,
        scratch_shapes=[
            pltpu.VMEM(value.shape, BF16),
            *(pltpu.VMEM(t.shape, BF16) for t in consts),
            pltpu.VMEM((1, channels), F32),
            pltpu.VMEM(value.shape, BF16),
            pltpu.VMEM((3, batch, rows, channels), BF16),
            pltpu.VMEM((4, count, proj.shape[0], half), BF16),
            pltpu.VMEM((batch * rows, channels), BF16),
            pltpu.VMEM((3, 2 * rows, channels), F32),
            pltpu.VMEM((2 * rows, channels), F32),
            pltpu.VMEM(filters.shape, F32),
            pltpu.VMEM(taps.shape, F32),
            pltpu.VMEM(value.shape, BF16),
            pltpu.VMEM(value.shape, BF16),
            pltpu.VMEM((2, batch * rows, half), BF16),
            pltpu.VMEM((2, batch * rows, half), BF16),
            pltpu.VMEM((2, batch, rows, half), BF16),
            pltpu.VMEM((2, batch, rows, half), BF16),
            dma((10,)),
            dma((2,)),
            dma((4,)),
            dma((batch,)),
            dma((batch,)),
        ]
        + [dma((batch,))] * 8
        + [dma((4, slots))] * 4
        + [dma((2,))] * 4,
        compiler_params=pltpu.CompilerParams(
            collective_id=0, has_side_effects=True, vmem_limit_bytes=67043328
        ),
    )(value, proj, *consts, skip[None], filters, taps, gate_in, gate_out)


def per_device(value, gate_in, gate_out, filters, skip, proj, taps):
    batch, rows, channels = value.shape
    assert filters.shape[0] % rows == 0 and taps.shape[0] <= rows
    count = filters.shape[0] // rows
    if (
        lax.axis_size("chan") == 2
        and lax.axis_size("ctx") % 4 == 0
        and (batch, count) == (2, 3)
        and taps.shape[0] == rows
        and proj.shape[0] % 16 == 0
        and channels % 512 == 0
    ):
        return fused(value, gate_in, gate_out, filters, skip, proj, taps)
    tile = min(256, channels)
    consts = [jnp.asarray(t) for t in tables(rows)]
    gathered = lax.all_gather(proj, "ctx", axis=0, tiled=True)
    blocks = [value] + [from_behind(value, s) for s in range(1, count + 1)]
    mixed = tiled(
        mix_kernel, consts, [filters, skip[None]], [gate_in, *blocks], tile, 4 * 10**9
    )
    partial = mm(mixed.reshape(batch * rows, channels), gathered)
    groups = lax.axis_size("chan")
    me = lax.axis_index("chan")
    width = partial.shape[1] // groups

    def columns(owner):
        return lax.dynamic_slice_in_dim(partial, owner * width, width, axis=1)

    total = columns(me)
    for step in range(1, groups):
        pairs = [(s, (s + step) % groups) for s in range(groups)]
        total = total + lax.ppermute(
            columns((me + step) % groups).astype(BF16), "chan", pairs
        ).astype(F32)
    projected = total.astype(BF16).reshape(batch, rows, width)
    behind = from_behind(projected, 1)
    return tiled(filter_kernel, consts, [taps], [gate_out, behind, projected], tile, 2 * 10**9)


def solution(mesh):
    in_specs = (
        P(None, "ctx", "chan"),
        P(None, "ctx", "chan"),
        P(None, "ctx", "chan"),
        P(None, "chan"),
        P("chan"),
        P(("chan", "ctx"), None),
        P(None, "chan"),
    )
    out_specs = P(None, "ctx", "chan")
    return jax.shard_map(
        per_device, mesh=mesh, in_specs=in_specs, out_specs=out_specs, check_vma=False
    )
```

profile of v0, /device:TPU:24, one launch (start us, length us, event | category | flops | bytes accessed | tf_op | source)
XLA Modules:
  0.0 60.5 jit_solution(7498561725743941719)
XLA Ops:
  0.0 58.6 %shard_map.109 = bf16[2,128,1024]{2,1,0:T(8,128)(2,1)} custom-call(bf16[2,128,1024]{2,1,0:T(8,128)(2,1)} %value_any.1, bf16[64,2048]{1,0:T(8,128)(2,1)} %proj_any.1, bf16[256,256]{1,0:T(8,128)(2,1)} %constant.8.clone.fh_any, bf16[256,256]{1,0:T(8,128)(2,1)} %constant.9.clone.fl_any, bf16[128,256]{1,0:T(8,128)(2,1)} %constant.10.clone.ih_any, ...), custom_call_target="tpu_custom_call" | custom-call | tf_op jit(solution)/shard_map/pallas_call | solution.py:510
  58.6 1.9 %copy.13 = bf16[2,128,1024]{2,1,0:T(8,128)(2,1)} copy(bf16[2,128,1024]{2,1,0:T(8,128)(2,1)} %shard_map.109) | data formatting | bytes 1048576
where the time goes:
time: 60.9 us; the launch traced here: 60.5 us
  Pallas kernels  58.6 us (96%)
  local copies, waits for them, and re-layouts  1.87 us (3%)
    pallas_call x1, Pallas kernels, fused(): pl.pallas_call(fused_kernel, out_shape=jax.ShapeDtypeStruct(value.shape,...  58.6 us
    unnamed x1, local copies, waits for them, and re-layouts  1.87 us

commit v1 on v0

--- a/solution.py
+++ b/solution.py
@@ -111,23 +111,26 @@
 MESH = pl.DeviceIdType.MESH
 
 
+UNITS = 4
+
+
 def fused_kernel(
     value_any, proj_any, fh_any, fl_any, ih_any, il_any, skip_any, filters_any, taps_any,
     gate_in_any, gate_out_any,
     out_any,
     value, fh, fl, ih, il, skip, out,
     past, gathered, mixed, spectra, tap_spectra, filters, taps, gate_in, gate_out,
-    x_send, x_recv, own_rows, rim,
+    own_rows, rim,
     load_sem, store_sem, own_sem, back_send, back_recv, halo_send, halo_recv, relay_send, relay_recv, far_send, far_recv,
-    near_send, near_recv, ring_send, ring_recv, share_send, share_recv,
-    x_send_sem, x_recv_sem, rim_send, rim_recv,
+    near_send, near_recv, ring_send, ring_recv, share_send, share_recv, first_send, first_recv,
+    swap_send, swap_recv, mixed_send, mixed_recv, rim_send, rim_recv,
 ):
     batch, rows, channels = value.shape
     count = lax.axis_size("ctx")
     chips = count // 2
     evens = chips // 2
-    half = gathered.shape[-1]
-    tile = min(256, half)
+    width = gathered.shape[-1]
+    tile = min(256, width)
     me, j = lax.axis_index("chan"), lax.axis_index("ctx")
     chip, core = j // 2, j % 2
     sibling = chip * 2 + 1 - core
@@ -159,14 +162,12 @@
     for load in loads:
         load.start()
 
-    def columns(unit):
-        owner = partner if unit < 2 else me
-        start = owner * (2 * half) + (unit % 2) * half
-        return pl.ds(pl.multiple_of(start, half), half)
+    def columns(owner, unit):
+        return pl.ds(pl.multiple_of(owner * channels + unit * width, width), width)
 
     own_copies = [
-        pltpu.make_async_copy(proj_any.at[:, columns(q)], gathered.at[q, j], own_sem.at[q])
-        for q in range(4)
+        pltpu.make_async_copy(proj_any.at[:, columns(me, q)], gathered.at[q, me, j], own_sem.at[q])
+        for q in range(UNITS)
     ]
     for copy in own_copies:
         copy.start()
@@ -241,76 +242,96 @@
 
     reach = chips // 2
 
-    def steps(unit, direction):
-        return reach if direction == 1 else chips - 1 - reach
+    def swap(unit):
+        return remote(
+            proj_any.at[:, columns(partner, unit)],
+            gathered.at[unit, me, j],
+            swap_send.at[unit],
+            swap_recv.at[unit],
+            (partner, j),
+        )
+
+    def piece(unit, direction, step, origin):
+        if step < reach:
+            return gathered.at[unit, :, origin]
+        return gathered.at[unit, 0 if direction == 1 else 1, origin]
 
     def slot(direction, step):
-        return step if direction == 1 else reach + step
+        return step - 1 if direction == 1 else reach + step - 1
 
     def hop(unit, direction, step):
         origin = holder(place - direction * (step - 1))
-        source = proj_any.at[:, columns(unit)] if step == 1 else gathered.at[unit, origin]
         k = slot(direction, step)
+        moved = piece(unit, direction, step, origin)
         return remote(
-            source,
-            gathered.at[unit, origin],
+            moved,
+            moved,
             ring_send.at[unit, k],
             ring_recv.at[unit, k],
             (me, following if direction == 1 else preceding),
         )
 
-    def share(unit, direction, step):
+    def share(unit, direction, step, other=False):
         origin = holder(place - direction * step)
-        k = slot(direction, step) if step else 0
-        source = gathered.at[unit, origin] if step else proj_any.at[:, columns(unit)]
+        if other:
+            origin = origin + 1 - 2 * core
+        k = slot(direction, step)
+        moved = piece(unit, direction, step, origin)
         return remote(
-            source,
-            gathered.at[unit, origin],
-            share_send.at[unit, k],
-            share_recv.at[unit, k],
-            (me, sibling),
-        )
+            moved, moved, share_send.at[unit, k], share_recv.at[unit, k], (me, sibling)
+        )
+
+    def share_own(unit, other=False):
+        moved = gathered.at[unit, :, sibling if other else j]
+        return remote(moved, moved, first_send.at[unit], first_recv.at[unit], (me, sibling))
 
     hops = {}
 
-    def send_step(units, step):
-        for unit in units:
+    def wave(unit, step):
+        if step == 1:
+            own_copies[unit].wait()
+            swaps[unit].wait_recv()
+        for direction in (1, -1):
+            if step > 1:
+                hops[unit, direction, step - 1].wait_recv()
+            if step <= reach:
+                copy = hops[unit, direction, step] = hop(unit, direction, step)
+                begin(copy)
+        if step == 1:
+            begin(share_own(unit))
+        else:
             for direction in (1, -1):
-                if step > 1 and step - 1 <= steps(unit, direction):
-                    arrived = hops[unit, direction, step - 1]
-                    arrived.wait_recv()
-                if step <= steps(unit, direction):
-                    copy = hops[unit, direction, step] = hop(unit, direction, step)
-                    begin(copy)
-                if step > 1 and step - 1 <= steps(unit, direction):
-                    begin(share(unit, direction, step - 1))
+                begin(share(unit, direction, step - 1))
 
     def finish(unit):
-        own_copies[unit].wait()
-        share(unit, 1, 0).wait_recv()
+        share_own(unit, other=True).wait_recv()
         for direction in (1, -1):
-            for step in range(1, steps(unit, direction) + 1):
-                k_origin = holder(place - direction * step)
-                other = k_origin + 1 - 2 * core
-                k = slot(direction, step)
-                remote(
-                    gathered.at[unit, other],
-                    gathered.at[unit, other],
-                    share_send.at[unit, k],
-                    share_recv.at[unit, k],
-                    (me, sibling),
-                ).wait_recv()
+            for step in range(1, reach + 1):
+                share(unit, direction, step, other=True).wait_recv()
 
     def product(unit):
-        table = gathered[unit].reshape(count * proj_any.shape[0], half)
-        return mm(mixed[...], table)
-
+        total = None
+        for plane in range(2):
+            table = gathered[unit, plane].reshape(count * proj_any.shape[0], width)
+            part = mm(mixed[plane].reshape(batch * rows, channels), table)
+            total = part if total is None else total + part
+        return total
+
+    swaps = [swap(unit) for unit in range(UNITS)]
+    for copy in swaps:
+        begin(copy)
     start_halo(0)
-    send_step((0, 1), 1)
+    wave(0, 1)
+    wave(1, 1)
     start_halo(1)
-    send_step((2, 3), 1)
-    for unit in range(4):
-        begin(share(unit, 1, 0))
+    wave(2, 1)
+    wave(3, 1)
+    waves = [(unit, step) for step in range(2, reach + 2) for unit in range(UNITS)]
+
+    def pump(number):
+        for _ in range(number):
+            if waves:
+                wave(*waves.pop(0))
 
     table_refs = (fh, fl, ih, il)
     for load in (loads[0], *loads[4:]):
@@ -360,9 +381,9 @@
             relay(b, 0).start()
 
     relay_halo(0)
-    send_step((0, 1), 2)
+    pump(2)
     relay_halo(1)
-    send_step((2, 3), 2)
+    pump(2)
     loads[2].wait()
 
     def mix(b):
@@ -386,13 +407,23 @@
             conv = convolve(windows, [spectra.at[s, :, at][...] for s in range(3)], table_refs)
             both = conv + skip[:, at] * parts[0].astype(F32)
             gated = gate_in[b, :, at].astype(F32) * both
-            mixed[b * rows : (b + 1) * rows, at] = gated.astype(BF16)
+            mixed[me, b, :, at] = gated.astype(BF16)
+
+    def trade(b):
+        return remote(
+            mixed.at[me, b], mixed.at[me, b], mixed_send.at[b], mixed_recv.at[b], (partner, j)
+        )
+
+    def traded(b):
+        moved = mixed.at[partner, b]
+        return remote(moved, moved, mixed_send.at[b], mixed_recv.at[b], (partner, j))
 
     mix(0)
-    send_step((0, 1), 3)
+    begin(trade(0))
+    pump(2)
     mix(1)
-    send_step((2, 3), 3)
-    send_step((0, 1), 4)
+    begin(trade(1))
+    pump(4)
     loads[1].wait()
 
     @pl.loop(0, channels // tile)
@@ -400,73 +431,55 @@
         at = pl.ds(pl.multiple_of(i * tile, tile), tile)
         tap_spectra[:, at] = lag_spectrum(taps[:, at], fh[...], fl[...])
 
-    x_copies = []
-    send_step((2, 3), 4)
-    for step in range(5, reach + 2):
-        send_step((0, 1), step)
-    for unit in range(2):
-        finish(unit)
-        x_send[unit] = product(unit).astype(BF16)
-        copy = remote(
-            x_send.at[unit],
-            x_recv.at[unit],
-            x_send_sem.at[unit],
-            x_recv_sem.at[unit],
-            (partner, j),
-        )
-        x_copies.append(copy)
-        begin(copy)
-    for step in range(5, reach + 2):
-        send_step((2, 3), step)
-
     @pl.when(j == 0)
     def _():
         rim[...] = jnp.zeros(rim.shape, BF16)
 
-    def edge(h):
+    loads[3].wait()
+
+    def edge(u):
         return remote(
-            own_rows.at[h], rim.at[h], rim_send.at[h], rim_recv.at[h], (me, j + 1)
-        )
-
-    for h in range(2):
-        finish(2 + h)
-        partial = product(2 + h)
-        x_copies[h].wait_recv()
-        total = (partial + x_recv[h].astype(F32)).astype(BF16)
-        own_rows[h] = total.reshape(batch, rows, half)
+            own_rows.at[u], rim.at[u], rim_send.at[u], rim_recv.at[u], (me, j + 1)
+        )
+
+    def store(u):
+        part = pl.ds(u * width, width)
+        return pltpu.make_async_copy(
+            out.at[:, :, part], out_any.at[:, :, part], store_sem.at[u]
+        )
+
+    def emit(u):
+        @pl.when(j >= 1)
+        def _():
+            edge(u).wait_recv()
+
+        wide = pl.ds(u * width, width)
+        spectrum = tap_spectra[:, wide]
+        for b in range(batch):
+            window = jnp.concatenate([rim[u, b], own_rows[u, b]], axis=0)
+            shorted = convolve([window], [spectrum], table_refs)
+            out[b, :, wide] = (gate_out[b, :, wide].astype(F32) * shorted).astype(BF16)
+        store(u).start()
+
+    for u in range(UNITS):
+        while any(w[0] == u for w in waves):
+            pump(1)
+        finish(u)
+        if u == 0:
+            for b in range(batch):
+                traded(b).wait_recv()
+        own_rows[u] = product(u).astype(BF16).reshape(batch, rows, width)
 
         @pl.when(j + 1 < count)
-        def _(h=h):
-            edge(h).start()
-
-    loads[3].wait()
-
-    def store(h):
-        part = pl.ds(h * half, half)
-        return pltpu.make_async_copy(
-            out.at[:, :, part], out_any.at[:, :, part], store_sem.at[h]
-        )
-
-    for h in range(2):
-
-        @pl.when(j >= 1)
-        def _(h=h):
-            edge(h).wait_recv()
-
-        @pl.loop(0, half // tile)
-        def _(i, h=h):
-            at = pl.ds(pl.multiple_of(i * tile, tile), tile)
-            wide = pl.ds(pl.multiple_of(h * half + i * tile, tile), tile)
-            spectrum = tap_spectra[:, wide]
-            for b in range(batch):
-                window = jnp.concatenate([rim[h, b, :, at], own_rows[h, b, :, at]], axis=0)
-                shorted = convolve([window], [spectrum], table_refs)
-                out[b, :, wide] = (gate_out[b, :, wide].astype(F32) * shorted).astype(BF16)
-
-        store(h).start()
-
-    for h in range(2):
-        store(h).wait()
+        def _(u=u):
+            edge(u).start()
+
+        if u:
+            emit(u - 1)
+    emit(UNITS - 1)
+
+    for u in range(UNITS):
+        store(u).wait()
     for copy in sent:
         copy.wait_send()
 
@@ -492,19 +505,19 @@
         def _(b=b):
             back(b).wait_send()
 
-    for h in range(2):
+    for u in range(UNITS):
 
         @pl.when(j + 1 < count)
-        def _(h=h):
-            edge(h).wait_send()
+        def _(u=u):
+            edge(u).wait_send()
 
 
 def fused(value, gate_in, gate_out, filters, skip, proj, taps):
     batch, rows, channels = value.shape
     count = lax.axis_size("ctx")
     consts = [jnp.asarray(t) for t in tables(rows)]
-    half = channels // 2
-    slots = 2 * (count // 4) + 1
+    width = channels // UNITS
+    slots = 2 * (count // 4)
     dma = pltpu.SemaphoreType.DMA
     anywhere = pl.BlockSpec(memory_space=pl.ANY)
     return pl.pallas_call(
@@ -518,27 +531,27 @@
             pltpu.VMEM((1, channels), F32),
             pltpu.VMEM(value.shape, BF16),
             pltpu.VMEM((3, batch, rows, channels), BF16),
-            pltpu.VMEM((4, count, proj.shape[0], half), BF16),
-            pltpu.VMEM((batch * rows, channels), BF16),
+            pltpu.VMEM((UNITS, 2, count, proj.shape[0], width), BF16),
+            pltpu.VMEM((2, batch, rows, channels), BF16),
             pltpu.VMEM((3, 2 * rows, channels), F32),
             pltpu.VMEM((2 * rows, channels), F32),
             pltpu.VMEM(filters.shape, F32),
             pltpu.VMEM(taps.shape, F32),
             pltpu.VMEM(value.shape, BF16),
             pltpu.VMEM(value.shape, BF16),
-            pltpu.VMEM((2, batch * rows, half), BF16),
-            pltpu.VMEM((2, batch * rows, half), BF16),
-            pltpu.VMEM((2, batch, rows, half), BF16),
-            pltpu.VMEM((2, batch, rows, half), BF16),
+            pltpu.VMEM((UNITS, batch, rows, width), BF16),
+            pltpu.VMEM((UNITS, batch, rows, width), BF16),
             dma((10,)),
-            dma((2,)),
-            dma((4,)),
+            dma((UNITS,)),
+            dma((UNITS,)),
             dma((batch,)),
             dma((batch,)),
         ]
         + [dma((batch,))] * 8
-        + [dma((4, slots))] * 4
-        + [dma((2,))] * 4,
+        + [dma((UNITS, slots))] * 4
+        + [dma((UNITS,))] * 4
+        + [dma((batch,))] * 2
+        + [dma((UNITS,))] * 2,
         compiler_params=pltpu.CompilerParams(
             collective_id=0, has_side_effects=True, vmem_limit_bytes=67043328
         ),

time: 60.9 us -> 56.8 us (0.933)
  Pallas kernels: 58.6 us -> 54.8 us
    pallas_call x1, Pallas kernels: 58.6 us -> 54.8 us  [fused(): pl.pallas_call(fused_kernel, out_shape=jax.ShapeDtypeStruct(value.shape,...]
where the time goes in v1:
time: 56.8 us; the launch traced here: 56.7 us
  Pallas kernels  54.8 us (96%)
  local copies, waits for them, and re-layouts  1.87 us (3%)
    pallas_call x1, Pallas kernels, fused(): pl.pallas_call(fused_kernel, out_shape=jax.ShapeDtypeStruct(value.shape,...  54.8 us
    unnamed x1, local copies, waits for them, and re-layouts  1.87 us

profile of v1, /device:TPU:24, one launch (start us, length us, event | category | flops | bytes accessed | tf_op | source)
XLA Modules:
  0.0 56.7 jit_solution(3786077745501205796)
XLA Ops:
  0.0 54.8 %shard_map.109 = bf16[2,128,1024]{2,1,0:T(8,128)(2,1)} custom-call(bf16[2,128,1024]{2,1,0:T(8,128)(2,1)} %value_any.1, bf16[64,2048]{1,0:T(8,128)(2,1)} %proj_any.1, bf16[256,256]{1,0:T(8,128)(2,1)} %constant.8.clone.fh_any, bf16[256,256]{1,0:T(8,128)(2,1)} %constant.9.clone.fl_any, bf16[128,256]{1,0:T(8,128)(2,1)} %constant.10.clone.ih_any, ...), custom_call_target="tpu_custom_call" | custom-call | tf_op jit(solution)/shard_map/pallas_call | solution.py:523
  54.8 1.9 %copy.13 = bf16[2,128,1024]{2,1,0:T(8,128)(2,1)} copy(bf16[2,128,1024]{2,1,0:T(8,128)(2,1)} %shard_map.109) | data formatting | bytes 1048576

commit v2 on v1

--- a/solution.py
+++ b/solution.py
@@ -43,18 +43,17 @@
 
 
 def convolve(windows, spectra, table_refs):
-    fwd_hi, fwd_lo, inv_hi, inv_lo = table_refs
+    forward, inverse = table_refs[0], table_refs[2]
     total_re = total_im = None
     for window, spectrum in zip(windows, spectra):
-        seen = mm(fwd_hi[...], window) + mm(fwd_lo[...], window)
+        seen = mm(forward[...], window)
         half = seen.shape[0] // 2
         x_re, x_im, h_re, h_im = seen[:half], seen[half:], spectrum[:half], spectrum[half:]
         re = x_re * h_re - x_im * h_im
         im = x_re * h_im + x_im * h_re
         total_re = re if total_re is None else total_re + re
         total_im = im if total_im is None else total_im + im
-    high, low = split(jnp.concatenate([total_re, total_im], axis=0))
-    return mm(inv_hi[...], high) + mm(inv_hi[...], low) + mm(inv_lo[...], high)
+    return mm(inverse[...], jnp.concatenate([total_re, total_im], axis=0).astype(BF16))
 
 
 def mix_kernel(fh, fl, ih, il, filters, skip, gate, *rest):
@@ -461,6 +460,7 @@
             out[b, :, wide] = (gate_out[b, :, wide].astype(F32) * shorted).astype(BF16)
         store(u).start()
 
+    pump(len(waves))
     for u in range(UNITS):
         while any(w[0] == u for w in waves):
             pump(1)

time: 56.8 us -> 52.4 us (0.923)
  Pallas kernels: 54.8 us -> 49.9 us
    pallas_call x1, Pallas kernels: 54.8 us -> 49.9 us  [fused(): pl.pallas_call(fused_kernel, out_shape=jax.ShapeDtypeStruct(value.shape,...]
where the time goes in v2:
time: 52.4 us; the launch traced here: 51.8 us
  Pallas kernels  49.9 us (95%)
  local copies, waits for them, and re-layouts  1.87 us (4%)
    pallas_call x1, Pallas kernels, fused(): pl.pallas_call(fused_kernel, out_shape=jax.ShapeDtypeStruct(value.shape,...  49.9 us
    unnamed x1, local copies, waits for them, and re-layouts  1.87 us

profile of v2, /device:TPU:24, one launch (start us, length us, event | category | flops | bytes accessed | tf_op | source)
XLA Modules:
  0.0 51.8 jit_solution(17732847819202274254)
XLA Ops:
  0.0 49.9 %shard_map.109 = bf16[2,128,1024]{2,1,0:T(8,128)(2,1)} custom-call(bf16[2,128,1024]{2,1,0:T(8,128)(2,1)} %value_any.1, bf16[64,2048]{1,0:T(8,128)(2,1)} %proj_any.1, bf16[256,256]{1,0:T(8,128)(2,1)} %constant.8.clone.fh_any, bf16[256,256]{1,0:T(8,128)(2,1)} %constant.9.clone.fl_any, bf16[128,256]{1,0:T(8,128)(2,1)} %constant.10.clone.ih_any, ...), custom_call_target="tpu_custom_call" | custom-call | tf_op jit(solution)/shard_map/pallas_call | solution.py:523
  49.9 1.9 %copy.13 = bf16[2,128,1024]{2,1,0:T(8,128)(2,1)} copy(bf16[2,128,1024]{2,1,0:T(8,128)(2,1)} %shard_map.109) | data formatting | bytes 1048576
